TPU v7x, 32 devices: a whole 2x2x4 slice. The times are simulated.
32 devices in a mesh: dp: 8 (over y, x, core), tp: 4 (over z).
Axes of the slice: x: 2, y: 2, z: 4, core: 2. Of those that a mesh axis runs over, the one named last changes fastest.
Arguments:
- inputs: bfloat16 [26624, 768], P(('dp', 'tp')), may hold values from -6 to 6
- segment_ids: int32 [32, 832], P('dp'), may hold values from -1 to 4, as said below
- mask_flags: int32 [32, 832], P(('dp', 'tp')), may hold values 0 or 1
- mask_token: bfloat16 [768], replicated, may hold values from -6 to 6
- norm_gain: bfloat16 [768], replicated, may hold values from 0.5 to 1.5
- norm_shift: bfloat16 [768], replicated, may hold values from -3 to 3
- heads_weight: bfloat16 [768, 12, 192], P(None, 'tp'), may hold values from -0.21875 to 0.21875
- heads_bias: bfloat16 [12, 128], P('tp'), may hold values from -1.1953125 to 1.1953125
- proj_weight: bfloat16 [768, 768], P('tp'), may hold values from -1.75 to 1.75
- proj_bias: bfloat16 [768], replicated, may hold values from -2 to 2
- attn_scale: bfloat16 [768], replicated, may hold values from 0.5 to 1.5
- mlp_gain: bfloat16 [768], replicated, may hold values from 0.5 to 1.5
- mlp_shift: bfloat16 [768], replicated, may hold values from -3 to 3
- up_weight: bfloat16 [768, 3072], P(None, 'tp'), may hold values from -0.21875 to 0.21875
- up_bias: bfloat16 [3072], P('tp'), may hold values from -2 to 2
- down_weight: bfloat16 [3072, 768], P('tp'), may hold values from -0.109375 to 0.109375
- down_bias: bfloat16 [768], replicated, may hold values from -2 to 2
- mlp_scale: bfloat16 [768], replicated, may hold values from 0.5 to 1.5
- grad_out: bfloat16 [26624, 768], P(('dp', 'tp')), may hold values from -6 to 6
Outputs:
- output: bfloat16 [26624, 768], P(('dp', 'tp'))
- grad_inputs: float32 [26624, 768], P(('dp', 'tp'))
- grad_token: float32 [768], replicated
- grad_norm_gain: float32 [768], replicated
- grad_norm_shift: float32 [768], replicated
- grad_heads_weight: float32 [768, 12, 192], P(None, 'tp')
- grad_heads_bias: float32 [12, 128], P('tp')
- grad_proj_weight: float32 [768, 768], P('tp')
- grad_proj_bias: float32 [768], replicated
- grad_attn_scale: float32 [768], replicated
- grad_mlp_gain: float32 [768], replicated
- grad_mlp_shift: float32 [768], replicated
- grad_up_weight: float32 [768, 3072], P(None, 'tp')
- grad_up_bias: float32 [3072], P('tp')
- grad_down_weight: float32 [3072, 768], P('tp')
- grad_down_bias: float32 [768], replicated
- grad_mlp_scale: float32 [768], replicated
Inputs may be any that keep to these rules, and one draw needn't show every extreme that they name: `segment_ids`: every packed row holds five images numbered 0 to 4 in order from its first slot, then 1 to 32 padding slots marked -1 at its end; each of the first four images has h * w + 1 slots with h and w from 11 to 14, the fifth fills the rest.
All inputs are finite; a program needn't handle non-finite values. No bound on the sum of `mask_flags` on one device may be relied on, other than what follows from the above.
Results may differ from a plain program's by a relative error of at most 0.02.
Values may be sent and summed in bfloat16 or wider, within the bound.
A program may use at most 192 MiB of HBM per device.

v0:
```python
import functools
import jax
import jax.numpy as jnp
from jax import lax
from jax.sharding import PartitionSpec as P

EPSILON = 1e-06
FLOOR_SCORE = -1e30
SQRT_HALF = 0.7071067811865476
INV_ROOT_TWO_PI = 0.3989422804014327


def layer_norm(values, gain, shift):
    centre = values - jnp.mean(values, axis=-1, keepdims=True)
    inverse = lax.rsqrt(jnp.mean(centre * centre, axis=-1, keepdims=True) + EPSILON)
    scaled = centre * inverse
    return (scaled * gain + shift, scaled, inverse)


def norm_back(grad_normed, scaled, inverse, gain):
    grad_scaled = grad_normed * gain
    first = jnp.mean(grad_scaled, axis=-1, keepdims=True)
    second = jnp.mean(grad_scaled * scaled, axis=-1, keepdims=True)
    return inverse * (grad_scaled - first - scaled * second)


def gelu_parts(inner):
    normal_cdf = 0.5 * (1.0 + lax.erf(inner * SQRT_HALF))
    density = jnp.exp(-0.5 * inner * inner) * INV_ROOT_TWO_PI
    return (inner * normal_cdf, normal_cdf + inner * density)


def head_bias_row(bias, head_size):
    blank = jnp.zeros((bias.shape[0], head_size), jnp.float32)
    joined = jnp.concatenate(
        [bias[:, :head_size].astype(jnp.float32), blank, bias[:, head_size:].astype(jnp.float32)],
        axis=1,
    )
    return joined.reshape(-1)


def gather_weight(block, _):
    count = lax.axis_size("dp")
    rows = block.shape[0] // 8
    own = lax.dynamic_slice_in_dim(block, lax.axis_index("dp") % 8 * rows, rows, 0)
    if count == 8:
        return lax.all_gather(own, ("tp", "dp"), axis=0, tiled=True)
    return lax.all_gather(block, "tp", axis=0, tiled=True)


def scatter_grad(partial):
    part = lax.psum_scatter(partial, ("tp", "dp"), scatter_dimension=0, tiled=True)
    return lax.all_gather(part, "dp", axis=0, tiled=True).astype(jnp.float32)


def local(
    inputs,
    segment_ids,
    mask_flags,
    mask_token,
    norm_gain,
    norm_shift,
    heads_weight,
    heads_bias,
    proj_weight,
    proj_bias,
    attn_scale,
    mlp_gain,
    mlp_shift,
    up_weight,
    up_bias,
    down_weight,
    down_bias,
    mlp_scale,
    grad_out,
):
    own_rows, slots = mask_flags.shape
    width = inputs.shape[1]
    triple = heads_weight.shape[2]
    head_size = triple // 3
    scale = head_size ** (-0.5)
    own_ids = lax.dynamic_slice_in_dim(segment_ids, lax.axis_index("tp") * own_rows, own_rows, 0)
    valid = (own_ids.reshape(-1, 1) >= 0).astype(jnp.float32)
    flagged = (mask_flags.reshape(-1, 1) == 1).astype(jnp.float32)
    f32, bf16 = (jnp.float32, jnp.bfloat16)
    dot = functools.partial(lax.dot_general, preferred_element_type=f32)
    nn = (((1,), (0,)), ((), ()))
    nt = (((1,), (1,)), ((), ()))
    tn = (((0,), (0,)), ((), ()))
    heads_all = gather_weight(heads_weight.reshape(width, -1), width // 8)
    proj_all = gather_weight(proj_weight, 0)
    up_all = gather_weight(up_weight, 0)
    down_all = gather_weight(down_weight, 0)
    n_tp = lax.axis_size("tp")
    all_heads_bias = lax.all_gather(heads_bias.astype(f32), "tp", axis=0, tiled=True)
    up_bias_all = lax.all_gather(up_bias.astype(f32), "tp", axis=0, tiled=True)
    heads_now = all_heads_bias.shape[0]
    start_x = valid * (flagged * mask_token.astype(f32) + (1.0 - flagged) * inputs.astype(f32))
    first_gain = norm_gain.astype(f32)
    second_gain = mlp_gain.astype(f32)
    normed1, scaled1, inverse1 = layer_norm(start_x, first_gain, norm_shift.astype(f32))
    normed1 = normed1.astype(bf16)
    heads_cat = jnp.moveaxis(heads_all.reshape(n_tp, width, -1), 0, 1).reshape(width, -1)
    packed = (dot(normed1, heads_cat, nn) + head_bias_row(all_heads_bias, head_size)).astype(bf16)
    blocks = packed.reshape(slots, heads_now, triple)
    query = blocks[..., :head_size]
    keys = blocks[..., head_size : 2 * head_size]
    values = blocks[..., 2 * head_size :]
    groups = own_ids[0]
    same = (groups[:, None] == groups[None, :])[None]
    scores = jnp.einsum("qhd,khd->hqk", query, keys, preferred_element_type=f32) * scale
    scores = jnp.where(same, scores, FLOOR_SCORE)
    largest = jnp.max(scores, axis=-1, keepdims=True)
    raised = jnp.exp(scores - largest)
    total = jnp.sum(raised, axis=-1, keepdims=True)
    shares = (raised / total).astype(bf16)
    mixed = jnp.einsum("hqk,khd->qhd", shares, values, preferred_element_type=f32).astype(bf16)
    mixed = mixed.reshape(slots, -1)
    branch1 = dot(mixed, proj_all, nn) + proj_bias.astype(f32)
    middle = start_x + attn_scale.astype(f32) * branch1
    normed2, scaled2, inverse2 = layer_norm(middle, second_gain, mlp_shift.astype(f32))
    normed2 = normed2.astype(bf16)
    up_cat = jnp.moveaxis(up_all.reshape(n_tp, width, -1), 0, 1).reshape(width, -1)
    unit_input = dot(normed2, up_cat, nn) + up_bias_all
    unit_value, derivative = gelu_parts(unit_input)
    unit_low = unit_value.astype(bf16)
    branch2 = dot(unit_low, down_all, nn) + down_bias.astype(f32)
    output = (valid * (middle + mlp_scale.astype(f32) * branch2)).astype(bf16)
    grad_final = valid * grad_out.astype(f32)
    grad_scale2 = jnp.sum(branch2 * grad_final, axis=0)
    grad_branch2 = mlp_scale.astype(f32) * grad_final
    grad_down_bias = jnp.sum(grad_branch2, axis=0)
    grad_low2 = grad_branch2.astype(bf16)
    sum_down = scatter_grad(dot(unit_low, grad_low2, tn).astype(bf16))
    grad_unit = (dot(grad_low2, down_all, nt) * derivative).astype(bf16)
    columns = lambda g: jnp.moveaxis(g.reshape(width, n_tp, -1), 1, 0).reshape(n_tp * width, -1)
    sum_up = scatter_grad(columns(dot(normed2, grad_unit, tn).astype(bf16)))
    grad_up_bias = jnp.sum(grad_unit, axis=0, dtype=f32)
    grad_normed2 = dot(grad_unit, up_cat, nt)
    grad_gain2 = jnp.sum(grad_normed2 * scaled2, axis=0)
    grad_shift2 = jnp.sum(grad_normed2, axis=0)
    grad_middle = grad_final + norm_back(grad_normed2, scaled2, inverse2, second_gain)
    grad_scale1 = jnp.sum(branch1 * grad_middle, axis=0)
    grad_branch1 = attn_scale.astype(f32) * grad_middle
    grad_proj_bias = jnp.sum(grad_branch1, axis=0)
    grad_low1 = grad_branch1.astype(bf16)
    sum_proj = scatter_grad(dot(mixed, grad_low1, tn).astype(bf16))
    grad_mixed = dot(grad_low1, proj_all, nt).astype(bf16).reshape(slots, heads_now, head_size)
    exact = raised / total
    grad_shares = jnp.einsum("qhd,khd->hqk", grad_mixed, values, preferred_element_type=f32)
    centre = jnp.sum(exact * grad_shares, axis=-1, keepdims=True)
    grad_scores = (exact * (grad_shares - centre)).astype(bf16)
    grad_query = jnp.einsum("hqk,khd->qhd", grad_scores, keys, preferred_element_type=f32) * scale
    grad_keys = jnp.einsum("hqk,qhd->khd", grad_scores, query, preferred_element_type=f32) * scale
    grad_values = jnp.einsum("hqk,qhd->khd", shares, grad_mixed, preferred_element_type=f32)
    grad_packed = jnp.concatenate([grad_query, grad_keys, grad_values], axis=-1).astype(bf16)
    grad_packed = grad_packed.reshape(slots, -1)
    sum_heads = scatter_grad(columns(dot(normed1, grad_packed, tn).astype(bf16)))
    sum_heads = sum_heads.reshape(heads_weight.shape)
    bias_sums = jnp.sum(grad_packed, axis=0, dtype=f32).reshape(heads_now, triple)
    grad_normed1 = dot(grad_packed, heads_cat, nt)
    grad_gain1 = jnp.sum(grad_normed1 * scaled1, axis=0)
    grad_shift1 = jnp.sum(grad_normed1, axis=0)
    grad_start = grad_middle + norm_back(grad_normed1, scaled1, inverse1, first_gain)
    grad_inputs = valid * (1.0 - flagged) * grad_start
    grad_token = jnp.sum(valid * flagged * grad_start, axis=0)
    small = jnp.concatenate(
        [
            grad_token,
            grad_gain1,
            grad_shift1,
            grad_proj_bias,
            grad_scale1,
            grad_gain2,
            grad_shift2,
            grad_down_bias,
            grad_scale2,
            bias_sums.reshape(-1),
            grad_up_bias,
        ]
    )
    small = lax.psum(small, ("dp", "tp"))
    (
        sum_token,
        sum_gain1,
        sum_shift1,
        sum_proj_bias,
        sum_scale1,
        sum_gain2,
        sum_shift2,
        sum_down_bias,
        sum_scale2,
    ) = [small[i * width : (i + 1) * width] for i in range(9)]
    me = lax.axis_index("tp")
    bias_sums = small[9 * width : 9 * width + heads_now * triple].reshape(heads_now, triple)
    bias_sums = lax.dynamic_slice_in_dim(
        bias_sums, me * heads_bias.shape[0], heads_bias.shape[0], 0
    )
    sum_heads_bias = jnp.concatenate(
        [bias_sums[:, :head_size], bias_sums[:, 2 * head_size :]], axis=1
    )
    sum_up_bias = lax.dynamic_slice_in_dim(
        small[9 * width + heads_now * triple :], me * up_bias.shape[0], up_bias.shape[0], 0
    )
    return (
        output,
        grad_inputs,
        sum_token,
        sum_gain1,
        sum_shift1,
        sum_heads,
        sum_heads_bias,
        sum_proj,
        sum_proj_bias,
        sum_scale1,
        sum_gain2,
        sum_shift2,
        sum_up,
        sum_up_bias,
        sum_down,
        sum_down_bias,
        sum_scale2,
    )


def solution(mesh):
    placed = (
        P(("dp", "tp"), None),
        P("dp", None),
        P(("dp", "tp"), None),
        P(),
        P(),
        P(),
        P(None, "tp", None),
        P("tp", None),
        P("tp", None),
        P(),
        P(),
        P(),
        P(),
        P(None, "tp"),
        P("tp"),
        P("tp", None),
        P(),
        P(),
        P(("dp", "tp"), None),
    )
    return jax.shard_map(
        local,
        mesh=mesh,
        in_specs=placed,
        out_specs=(
            P(("dp", "tp"), None),
            P(("dp", "tp"), None),
            P(),
            P(),
            P(),
            P(None, "tp", None),
            P("tp", None),
            P("tp", None),
            P(),
            P(),
            P(),
            P(),
            P(None, "tp"),
            P("tp"),
            P("tp", None),
            P(),
            P(),
        ),
        check_vma=False,
    )
```

profile of v0, /device:TPU:0, one launch (start us, length us, event | category | flops | bytes accessed | tf_op | source)
XLA Modules:
  0.0 799.6 jit_solution(7235926682024903587)
XLA Ops:
  16.8 13.5 %all-gather = f32[4,3,128]{2,1,0:T(4,128)S(1)} all-gather(f32[1,3,128]{2,1,0:T(4,128)S(1)} %bitcast_convert_fusion), channel_id=1, replica_groups=mesh['dp'=8,'tp'=4] {'tp'}, dimensions={0}, use_global_device_ids=true | all-gather | bytes 7680 | tf_op jit(solution)/shard_map/all_gather | solution.py:95
  32.4 13.2 %all-gather.1 = f32[4,1,768]{2,1,0:T(1,128)S(1)} all-gather(f32[1,1,768]{2,1,0:T(1,128)S(1)} %reshape.247), channel_id=1, replica_groups=mesh['dp'=8,'tp'=4] {'tp'}, dimensions={0}, use_global_device_ids=true | all-gather | bytes 15360 | tf_op jit(solution)/shard_map/all_gather | solution.py:96
  45.6 30.0 %all-gather.9.cloned.1.call-done = bf16[3072,576]{1,0:T(8,128)(2,1)} async-done(((bf16[96,576]{1,0:T(8,128)(2,1)}), bf16[3072,576]{1,0:T(8,128)(2,1)}) %all-gather.9.cloned.1.call-update) | async-done | bytes 3538960 | tf_op jit(solution)/shard_map/all_gather | solution.py:47
  99.5 19.8 %fusion.53 = (f32[12,832]{1,0:T(8,128)S(1)}, f32[12,832,832]{1,2,0:T(8,128)}) fusion(pred[832,832]{0,1:T(8,128)(4,1)S(1)} %broadcast_compare_fusion, bf16[832,12,192]{0,2,1:T(8,128)(2,1)} %bitcast.56), kind=kOutput, calls=%fused_computation.116 | convolution fusion | flops 1096483584 | bytes 36711424 | tf_op jit(solution)/shard_map/sub | solution.py:114
  119.2 16.0 %fusion.26 = bf16[12,64,832]{2,1,0:T(8,128)(2,1)} fusion(bf16[832,12,192]{0,2,1:T(8,128)(2,1)} %bitcast.57, f32[12,832,832]{1,2,0:T(8,128)} %get-tuple-element.74, f32[12,832]{1,0:T(8,128)S(1)} %get-tuple-element.73), kind=kOutput, calls=%fused_computation.62 | convolution fusion | flops 1080508416 | bytes 38476800 | tf_op jit(solution)/shard_map/hqk,khd->qhd/dot_general | solution.py:117
  142.1 55.8 %all-gather.13.cloned.1.call-done = bf16[3072,768]{1,0:T(8,128)(2,1)} async-done(((bf16[96,768]{1,0:T(8,128)(2,1)}), bf16[3072,768]{1,0:T(8,128)(2,1)}) %all-gather.13.cloned.1.call-update) | async-done | bytes 4718608 | tf_op jit(solution)/shard_map/all_gather | solution.py:47
  204.5 10.7 %multiply_convert_fusion.1 = (bf16[832,3072]{1,0:T(8,128)(2,1)}, f32[832,3072]{1,0:T(8,128)}) fusion(f32[3072]{0:T(1024)S(1)} %bitcast.77, bf16[768,3072]{0,1:T(8,128)(2,1)} %bitcast.64, f32[832,768]{1,0:T(8,128)} %copy-done.4, f32[768]{0:T(1024)S(1)} %convert_element_type.165, f32[768]{0:T(1024)S(1)} %convert_element_type.164, f32[832]{0:T(1024)S(1)} %add_rsqrt_fusion, ...), kind=kOutput, calls=%fused_computation.18 | convolution fusion | flops 3944398848 | bytes 22635008 | tf_op jit(solution)/shard_map/dot_general | solution.py:124
  215.2 48.5 %all-gather.15.cloned.1.call-done = bf16[3072,768]{1,0:T(8,128)(2,1)} async-done(((bf16[96,768]{1,0:T(8,128)(2,1)}), bf16[3072,768]{1,0:T(8,128)(2,1)}) %all-gather.15.cloned.1.call-update) | async-done | bytes 4718608 | tf_op jit(solution)/shard_map/all_gather | solution.py:47
  263.7 11.2 %convert_reduce_fusion = (f32[3072]{0:T(1024)}, bf16[832,3072]{1,0:T(8,128)(2,1)S(1)}) fusion(f32[832,3072]{1,0:T(8,128)} %get-tuple-element.80, f32[3072]{0:T(1024)S(1)} %bitcast.78, bf16[3072,768]{1,0:T(8,128)(2,1)} %all-gather.15.cloned.1.call-done, bf16[832,768]{1,0:T(8,128)(2,1)S(1)} %copy-done.13, f32[768]{0:T(1024)S(1)} %convert_element_type.163, ...), kind=kOutput, calls=%fused_computation.17 | convolution fusion | flops 3961648128 | bytes 21362944 | tf_op jit(solution)/shard_map/dot_general | solution.py:135
  296.2 9.7 %reshape.241 = bf16[768,4,768]{2,1,0:T(4,128)(2,1)} reshape(bf16[768,3072]{1,0:T(8,128)(2,1)} %convolution_convert_fusion.1) | data formatting | bytes 9437184 | tf_op jit(solution)/shard_map/reshape | solution.py:136
  321.6 27.2 %multiply_reduce_fusion = (f32[12,832]{1,0:T(8,128)S(1)}, f32[12,832,832]{1,2,0:T(8,128)}) fusion(f32[12,832,832]{1,2,0:T(8,128)} %get-tuple-element.74, f32[12,832]{1,0:T(8,128)S(1)} %get-tuple-element.73, bf16[832,12,64]{0,2,1:T(8,128)(2,1)S(1)} %bitcast.74, bf16[832,12,192]{0,2,1:T(8,128)(2,1)} %bitcast.58), kind=kOutput, calls=%fused_computation.2 | convolution fusion | flops 1088166144 | bytes 71743488 | tf_op jit(solution)/shard_map/qhd,khd->hqk/dot_general | solution.py:150
  348.9 30.1 %multiply_convert_fusion = bf16[12,832,832]{1,2,0:T(8,128)(2,1)} fusion(f32[12,832,832]{1,2,0:T(8,128)} %get-tuple-element.78, f32[12,832]{1,0:T(8,128)S(1)} %get-tuple-element.77, f32[12,832,832]{1,2,0:T(8,128)} %get-tuple-element.74, f32[12,832]{1,0:T(8,128)S(1)} %get-tuple-element.73), kind=kLoop, calls=%fused_computation.1 | loop fusion | flops 33226752 | bytes 83146752 | tf_op jit(solution)/shard_map/convert_element_type | solution.py:152
  382.7 10.4 %multiply_bitcast_fusion = bf16[832,12,64]{0,2,1:T(8,128)(2,1)} fusion(bf16[12,832,832]{1,2,0:T(8,128)(2,1)} %multiply_convert_fusion, bf16[832,12,192]{0,2,1:T(8,128)(2,1)} %bitcast.59), kind=kOutput, calls=%fused_computation.31 | convolution fusion | flops 1064534016 | bytes 20545536 | tf_op jit(solution)/shard_map/hqk,qhd->khd/dot_general | solution.py:154
  393.1 15.3 %fusion.23 = bf16[832,12,64]{0,2,1:T(8,128)(2,1)} fusion(bf16[832,12,64]{0,2,1:T(8,128)(2,1)S(1)} %bitcast.75, f32[12,832,832]{1,2,0:T(8,128)} %get-tuple-element.74, f32[12,832]{1,0:T(8,128)S(1)} %get-tuple-element.73), kind=kOutput, calls=%fused_computation.61 | convolution fusion | flops 1079869440 | bytes 35822592 | tf_op jit(solution)/shard_map/hqk,qhd->khd/dot_general | solution.py:155
  408.5 10.0 %multiply_bitcast_fusion.1 = bf16[832,12,64]{0,2,1:T(8,128)(2,1)S(1)} fusion(bf16[12,832,832]{1,2,0:T(8,128)(2,1)} %multiply_convert_fusion, bf16[832,12,192]{0,2,1:T(8,128)(2,1)} %bitcast.60), kind=kOutput, calls=%fused_computation.32 | convolution fusion | flops 1064534016 | bytes 20545536 | tf_op jit(solution)/shard_map/hqk,khd->qhd/dot_general | solution.py:153
  440.8 9.7 %fusion.62 = f32[832,768]{1,0:T(8,128)} fusion(bf16[832,3072]{1,0:T(8,128)(2,1)} %get-tuple-element.79, bf16[3072,768]{1,0:T(8,128)(2,1)} %all-gather.15.cloned.1.call-done), kind=kOutput, calls=%fused_computation.117 | convolution fusion | flops 3925868544 | bytes 12386304 | tf_op jit(solution)/shard_map/dot_general | solution.py:127
  450.8 11.5 %multiply_reduce_fusion.4 = (f32[768]{0:T(1024)S(1)}, f32[832]{0:T(1024)S(1)}, f32[832]{0:T(1024)S(1)}, f32[768]{0:T(1024)S(1)}, f32[768]{0:T(1024)S(1)}, /*inde...) fusion(bf16[832,768]{1,0:T(8,128)(2,1)S(1)} %copy-done.3, f32[832]{0:T(1024)S(1)} %copy-done.30, ...), kind=kOutput, calls=%fused_computation.36 | convolution fusion | flops 2960371200 | bytes 18922240 | tf_op jit(solution)/shard_map/dot_general | solution.py:161
  465.3 64.1 %reduce-scatter.11.cloned.1.call-done = bf16[96,768]{1,0:T(8,128)(2,1)} async-done(((bf16[3072,768]{1,0:T(8,128)(2,1)}), bf16[96,768]{1,0:T(8,128)(2,1)}) %reduce-scatter.11.cloned.1.call-update) | async-done | bytes 147472 | tf_op jit(solution)/shard_map/reduce_scatter | solution.py:52
  529.6 40.5 %psum.7 = f32[12288]{0:T(1024)S(1)} all-reduce(f32[12288]{0:T(1024)S(1)} %constant_dynamic-update-slice_fusion), channel_id=1, replica_groups=mesh['dp'=8,'tp'=4] {'dp','tp'}, use_global_device_ids=true, to_apply=%region_22.23 | all-reduce | flops 12288 | bytes 98304 | tf_op jit(solution)/shard_map/psum | solution.py:182
  575.6 54.7 %reduce-scatter.7.cloned.1.call-done = bf16[24,768]{1,0:T(8,128)(2,1)} async-done(((bf16[768,768]{1,0:T(8,128)(2,1)}), bf16[24,768]{1,0:T(8,128)(2,1)}) %reduce-scatter.7.cloned.1.call-update) | async-done | bytes 36880 | tf_op jit(solution)/shard_map/reduce_scatter | solution.py:52
  640.8 98.1 %reduce-scatter.13.cloned.1.call-done = bf16[96,576]{1,0:T(8,128)(2,1)} async-done(((bf16[3072,576]{1,0:T(8,128)(2,1)}), bf16[96,576]{1,0:T(8,128)(2,1)}) %reduce-scatter.13.cloned.1.call-update) | async-done | bytes 110608 | tf_op jit(solution)/shard_map/reduce_scatter | solution.py:52
  738.8 10.8 %all_gather.36 = bf16[768,576]{1,0:T(8,128)(2,1)S(1)} all-gather(bf16[96,576]{1,0:T(8,128)(2,1)} %reduce-scatter.13.cloned.1.call-done), channel_id=1, replica_groups=mesh['dp'=8,'tp'=4] {'dp'}, dimensions={0}, use_global_device_ids=true | all-gather | bytes 995328 | tf_op jit(solution)/shard_map/all_gather | solution.py:53
  751.7 12.1 %all-gather.17.cloned.1.call-done = bf16[768,768]{1,0:T(8,128)(2,1)} async-done(((bf16[96,768]{1,0:T(8,128)(2,1)}), bf16[768,768]{1,0:T(8,128)(2,1)}) %all-gather.17.cloned.1.call-update) | async-done | bytes 1179664 | tf_op jit(solution)/shard_map/all_gather | solution.py:53
  766.7 22.9 %all-gather.19.cloned.1.call-done = bf16[768,768]{1,0:T(8,128)(2,1)} async-done(((bf16[96,768]{1,0:T(8,128)(2,1)}), bf16[768,768]{1,0:T(8,128)(2,1)}) %all-gather.19.cloned.1.call-update) | async-done | bytes 1179664 | tf_op jit(solution)/shard_map/all_gather | solution.py:53
  (216 shorter events, 138.5 us)
Async XLA Ops:
  7.3 68.2 %all-gather.9.cloned.1.call-start = ((), (), s32[]{:S(2)}) async-start(), calls=%async_computation.4 | async-start | bytes 4055040 | tf_op jit(solution)/shard_map/all_gather | solution.py:47
  9.4 125.8 %all-gather.11.cloned.1.call-start = ((), (), s32[]{:S(2)}) async-start(), calls=%async_computation.5 | async-start | bytes 1216512 | tf_op jit(solution)/shard_map/all_gather | solution.py:47
  10.9 187.0 %all-gather.13.cloned.1.call-start = ((), (), s32[]{:S(2)}) async-start(), calls=%async_computation.6 | async-start | bytes 4866048 | tf_op jit(solution)/shard_map/all_gather | solution.py:47
  11.7 252.0 %all-gather.15.cloned.1.call-start = ((), (), s32[]{:S(2)}) async-start(), calls=%async_computation.7 | async-start | bytes 4866048 | tf_op jit(solution)/shard_map/all_gather | solution.py:47
  13.3 437.2 %reduce-scatter.9.cloned.1.call-start = ((), (), s32[]{:S(2)}) async-start(), calls=%async_computation.9 | async-start | bytes 4866048 | tf_op jit(solution)/shard_map/reduce_scatter | solution.py:52
  14.1 121.2 %copy-start.16 = (f32[832]{0:T(1024)}, f32[832]{0:T(1024)S(1)}, u32[]{:S(2)}) copy-start(f32[832]{0:T(1024)S(1)} %convert_element_type.150) | copy-start | bytes 9988
  15.4 295.7 %copy-start.14 = (f32[832]{0:T(1024)}, f32[832]{0:T(1024)S(1)}, u32[]{:S(2)}) copy-start(f32[832]{0:T(1024)S(1)} %convert_element_type.149) | copy-start | bytes 9988
  16.0 119.2 %copy-start.18 = (f32[832]{0:T(1024)}, f32[832]{0:T(1024)S(1)}, u32[]{:S(2)}) copy-start(f32[832]{0:T(1024)S(1)} %get-tuple-element.72) | copy-start | bytes 9988
  16.6 118.7 %copy-start.20 = (f32[768]{0:T(1024)}, f32[768]{0:T(1024)S(1)}, u32[]{:S(2)}) copy-start(f32[768]{0:T(1024)S(1)} %convert_element_type.151) | copy-start | bytes 9220
  16.6 69.4 %copy-start.27 = (f32[768]{0:T(1024)}, f32[768]{0:T(1024)S(1)}, u32[]{:S(2)}) copy-start(f32[768]{0:T(1024)S(1)} %convert_element_type.154) | copy-start | bytes 9220
  16.7 272.4 %copy-start.33 = (f32[768]{0:T(1024)}, f32[768]{0:T(1024)S(1)}, u32[]{:S(2)}) copy-start(f32[768]{0:T(1024)S(1)} %convert_element_type.163) | copy-start | bytes 9220
  16.7 69.3 %copy-start.35 = (f32[768]{0:T(1024)}, f32[768]{0:T(1024)S(1)}, u32[]{:S(2)}) copy-start(f32[768]{0:T(1024)S(1)} %convert_element_type.155) | copy-start | bytes 9220
  204.5 70.3 %slice-start = ((s8[4718592]{0:T(1024)(128)(4,1)}), s8[524288]{0:T(1024)(128)(4,1)S(1)}, s32[]{:S(2)}) async-start(s8[4718592]{0:T(1024)(128)(4,1)} %bitcast.65), calls=%async_computation.14 | async-start | bytes 1048576
  311.1 218.3 %reduce-scatter.11.cloned.1.call-start = ((), (), s32[]{:S(2)}) async-start(), calls=%async_computation.11 | async-start | bytes 4866048 | tf_op jit(solution)/shard_map/reduce_scatter | solution.py:52
  348.8 281.6 %reduce-scatter.7.cloned.1.call-start = ((), (), s32[]{:S(2)}) async-start(), calls=%async_computation.8 | async-start | bytes 1216512 | tf_op jit(solution)/shard_map/reduce_scatter | solution.py:52
  408.5 330.4 %reduce-scatter.13.cloned.1.call-start = ((), (), s32[]{:S(2)}) async-start(), calls=%async_computation.13 | async-start | bytes 4055040 | tf_op jit(solution)/shard_map/reduce_scatter | solution.py:52
  440.0 323.8 %all-gather.17.cloned.1.call-start = ((), (), s32[]{:S(2)}) async-start(), calls=%async_computation.10 | async-start | bytes 1327104 | tf_op jit(solution)/shard_map/all_gather | solution.py:53
  450.5 339.1 %all-gather.19.cloned.1.call-start = ((), (), s32[]{:S(2)}) async-start(), calls=%async_computation.12 | async-start | bytes 1327104 | tf_op jit(solution)/shard_map/all_gather | solution.py:53
  462.3 67.1 %copy-start.25 = (f32[768]{0:T(1024)S(1)}, f32[768]{0:T(1024)}, u32[]{:S(2)}) copy-start(f32[768]{0:T(1024)} %get-tuple-element.42) | copy-start | bytes 9220
  462.3 67.1 %copy-start.24 = (f32[768]{0:T(1024)S(1)}, f32[768]{0:T(1024)}, u32[]{:S(2)}) copy-start(f32[768]{0:T(1024)} %get-tuple-element.41) | copy-start | bytes 9220
  462.3 67.1 %copy-start.38 = (f32[768]{0:T(1024)S(1)}, f32[768]{0:T(1024)}, u32[]{:S(2)}) copy-start(f32[768]{0:T(1024)} %get-tuple-element.34) | copy-start | bytes 9220
  462.3 67.2 %copy-start.37 = (f32[768]{0:T(1024)S(1)}, f32[768]{0:T(1024)}, u32[]{:S(2)}) copy-start(f32[768]{0:T(1024)} %get-tuple-element.40) | copy-start | bytes 9220
  462.4 67.2 %copy-start.32 = (f32[3072]{0:T(1024)S(1)}, f32[3072]{0:T(1024)}, u32[]{:S(2)}) copy-start(f32[3072]{0:T(1024)} %get-tuple-element.82) | copy-start | bytes 36868
  462.4 109.8 %copy-start.31 = (f32[832]{0:T(1024)S(1)}, f32[832]{0:T(1024)}, u32[]{:S(2)}) copy-start(f32[832]{0:T(1024)} %get-tuple-element.71) | copy-start | bytes 9988
  (40 other events, 472.0 us)
Sparse Core Ops, SparseCore 0:
  11.6 63.8 all-gather.8
  79.0 52.6 all-gather.10
  135.2 62.5 all-gather.12
  201.2 62.4 all-gather.14
  311.2 105.7 reduce-scatter.8
  423.3 106.0 reduce-scatter.10
  535.0 95.2 reduce-scatter.6
  635.8 103.0 reduce-scatter.12
  740.7 23.0 all-gather.16
  765.5 24.0 all-gather.18
where the time goes:
time: 804 us; the launch traced here: 800 us
  waiting for transfers between devices  386 us (48%)
  matrix products  186 us (23%)
  blocking collectives  87.6 us (11%)
  local copies, waits for them, and re-layouts  68.1 us (8%)
  other arithmetic  55.7 us (7%)
  between operations  15.4 us (2%)
    reduce_scatter x4, waiting for transfers between devices, scatter_grad(): lax.psum_scatter(partial, ('tp', 'dp'), scatter_dimension=0, tiled=True)  217 us
    all_gather x4, waiting for transfers between devices, gather_weight(): return lax.all_gather(own, ('tp', 'dp'), axis=0, tiled=True)  134 us
    psum x1, blocking collectives, local(): small = lax.psum(small, ('dp', 'tp'))  40.5 us
    all_gather x2, waiting for transfers between devices, scatter_grad(): return lax.all_gather(part, 'dp', axis=0, tiled=True).astype(jnp.float32)  35 us
    convert_element_type x1, other arithmetic, local(): grad_scores = (exact * (grad_shares - centre)).astype(bf16)  30.1 us
    dot_general x1, matrix products, local(): jnp.einsum('qhd,khd->hqk', grad_mixed, values, preferred_element_type=f32)  27.2 us
    all_gather x2, blocking collectives, scatter_grad(): return lax.all_gather(part, 'dp', axis=0, tiled=True).astype(jnp.float32)  20.4 us
    sub x1, matrix products, local(): raised = jnp.exp(scores - largest)  19.8 us
  transfers between devices with their start and end apart: 10, of which 8 were waited for; matrix products, arithmetic and copies ran while one was open for 31% of the time, Pallas kernels for 0%

commit v1 on v0

--- a/solution.py
+++ b/solution.py
@@ -179,7 +179,7 @@
             grad_up_bias,
         ]
     )
-    small = lax.psum(small, ("dp", "tp"))
+    small = lax.psum(lax.psum(small, "tp"), "dp")
     (
         sum_token,
         sum_gain1,

time: 804 us -> 804 us (level)
    psum x1 -> x2, blocking collectives: 40.5 us -> 41.2 us  [local(): small = lax.psum(lax.psum(small, 'tp'), 'dp')]
where the time goes in v1:
time: 804 us; the launch traced here: 800 us
  waiting for transfers between devices  386 us (48%)
  matrix products  186 us (23%)
  blocking collectives  88.3 us (11%)
  local copies, waits for them, and re-layouts  68.1 us (8%)
  other arithmetic  55.7 us (7%)
  between operations  15.4 us (2%)
    reduce_scatter x4, waiting for transfers between devices, scatter_grad(): lax.psum_scatter(partial, ('tp', 'dp'), scatter_dimension=0, tiled=True)  216 us
    all_gather x4, waiting for transfers between devices, gather_weight(): return lax.all_gather(own, ('tp', 'dp'), axis=0, tiled=True)  134 us
    psum x2, blocking collectives, local(): small = lax.psum(lax.psum(small, 'tp'), 'dp')  41.2 us
    all_gather x2, waiting for transfers between devices, scatter_grad(): return lax.all_gather(part, 'dp', axis=0, tiled=True).astype(jnp.float32)  35 us
    convert_element_type x1, other arithmetic, local(): grad_scores = (exact * (grad_shares - centre)).astype(bf16)  30.1 us
    dot_general x1, matrix products, local(): jnp.einsum('qhd,khd->hqk', grad_mixed, values, preferred_element_type=f32)  27.2 us
    all_gather x2, blocking collectives, scatter_grad(): return lax.all_gather(part, 'dp', axis=0, tiled=True).astype(jnp.float32)  20.3 us
    sub x1, matrix products, local(): raised = jnp.exp(scores - largest)  19.8 us
  transfers between devices with their start and end apart: 10, of which 8 were waited for; matrix products, arithmetic and copies ran while one was open for 31% of the time, Pallas kernels for 0%

profile of v1, /device:TPU:0, one launch (start us, length us, event | category | flops | bytes accessed | tf_op | source)
XLA Modules:
  0.0 799.6 jit_solution(3231710393818255993)
XLA Ops:
  16.8 13.5 %all-gather = f32[4,3,128]{2,1,0:T(4,128)S(1)} all-gather(f32[1,3,128]{2,1,0:T(4,128)S(1)} %bitcast_convert_fusion), channel_id=1, replica_groups=mesh['dp'=8,'tp'=4] {'tp'}, dimensions={0}, use_global_device_ids=true | all-gather | bytes 7680 | tf_op jit(solution)/shard_map/all_gather | solution.py:95
  32.4 13.2 %all-gather.1 = f32[4,1,768]{2,1,0:T(1,128)S(1)} all-gather(f32[1,1,768]{2,1,0:T(1,128)S(1)} %reshape.247), channel_id=1, replica_groups=mesh['dp'=8,'tp'=4] {'tp'}, dimensions={0}, use_global_device_ids=true | all-gather | bytes 15360 | tf_op jit(solution)/shard_map/all_gather | solution.py:96
  45.6 30.0 %all-gather.9.cloned.1.call-done = bf16[3072,576]{1,0:T(8,128)(2,1)} async-done(((bf16[96,576]{1,0:T(8,128)(2,1)}), bf16[3072,576]{1,0:T(8,128)(2,1)}) %all-gather.9.cloned.1.call-update) | async-done | bytes 3538960 | tf_op jit(solution)/shard_map/all_gather | solution.py:47
  99.5 19.8 %fusion.53 = (f32[12,832]{1,0:T(8,128)S(1)}, f32[12,832,832]{1,2,0:T(8,128)}) fusion(pred[832,832]{0,1:T(8,128)(4,1)S(1)} %broadcast_compare_fusion, bf16[832,12,192]{0,2,1:T(8,128)(2,1)} %bitcast.56), kind=kOutput, calls=%fused_computation.116 | convolution fusion | flops 1096483584 | bytes 36711424 | tf_op jit(solution)/shard_map/sub | solution.py:114
  119.3 16.0 %fusion.26 = bf16[12,64,832]{2,1,0:T(8,128)(2,1)} fusion(bf16[832,12,192]{0,2,1:T(8,128)(2,1)} %bitcast.57, f32[12,832,832]{1,2,0:T(8,128)} %get-tuple-element.74, f32[12,832]{1,0:T(8,128)S(1)} %get-tuple-element.73), kind=kOutput, calls=%fused_computation.62 | convolution fusion | flops 1080508416 | bytes 38476800 | tf_op jit(solution)/shard_map/hqk,khd->qhd/dot_general | solution.py:117
  142.1 55.8 %all-gather.13.cloned.1.call-done = bf16[3072,768]{1,0:T(8,128)(2,1)} async-done(((bf16[96,768]{1,0:T(8,128)(2,1)}), bf16[3072,768]{1,0:T(8,128)(2,1)}) %all-gather.13.cloned.1.call-update) | async-done | bytes 4718608 | tf_op jit(solution)/shard_map/all_gather | solution.py:47
  204.5 10.7 %multiply_convert_fusion.1 = (bf16[832,3072]{1,0:T(8,128)(2,1)}, f32[832,3072]{1,0:T(8,128)}) fusion(f32[3072]{0:T(1024)S(1)} %bitcast.77, bf16[768,3072]{0,1:T(8,128)(2,1)} %bitcast.64, f32[832,768]{1,0:T(8,128)} %copy-done.4, f32[768]{0:T(1024)S(1)} %convert_element_type.165, f32[768]{0:T(1024)S(1)} %convert_element_type.164, f32[832]{0:T(1024)S(1)} %add_rsqrt_fusion, ...), kind=kOutput, calls=%fused_computation.18 | convolution fusion | flops 3944398848 | bytes 22635008 | tf_op jit(solution)/shard_map/dot_general | solution.py:124
  215.2 48.5 %all-gather.15.cloned.1.call-done = bf16[3072,768]{1,0:T(8,128)(2,1)} async-done(((bf16[96,768]{1,0:T(8,128)(2,1)}), bf16[3072,768]{1,0:T(8,128)(2,1)}) %all-gather.15.cloned.1.call-update) | async-done | bytes 4718608 | tf_op jit(solution)/shard_map/all_gather | solution.py:47
  263.7 11.2 %convert_reduce_fusion = (f32[3072]{0:T(1024)}, bf16[832,3072]{1,0:T(8,128)(2,1)S(1)}) fusion(f32[832,3072]{1,0:T(8,128)} %get-tuple-element.80, f32[3072]{0:T(1024)S(1)} %bitcast.78, bf16[3072,768]{1,0:T(8,128)(2,1)} %all-gather.15.cloned.1.call-done, bf16[832,768]{1,0:T(8,128)(2,1)S(1)} %copy-done.13, f32[768]{0:T(1024)S(1)} %convert_element_type.163, ...), kind=kOutput, calls=%fused_computation.17 | convolution fusion | flops 3961648128 | bytes 21362944 | tf_op jit(solution)/shard_map/dot_general | solution.py:135
  296.2 9.7 %reshape.241 = bf16[768,4,768]{2,1,0:T(4,128)(2,1)} reshape(bf16[768,3072]{1,0:T(8,128)(2,1)} %convolution_convert_fusion.1) | data formatting | bytes 9437184 | tf_op jit(solution)/shard_map/reshape | solution.py:136
  321.6 27.2 %multiply_reduce_fusion = (f32[12,832]{1,0:T(8,128)S(1)}, f32[12,832,832]{1,2,0:T(8,128)}) fusion(f32[12,832,832]{1,2,0:T(8,128)} %get-tuple-element.74, f32[12,832]{1,0:T(8,128)S(1)} %get-tuple-element.73, bf16[832,12,64]{0,2,1:T(8,128)(2,1)S(1)} %bitcast.74, bf16[832,12,192]{0,2,1:T(8,128)(2,1)} %bitcast.58), kind=kOutput, calls=%fused_computation.2 | convolution fusion | flops 1088166144 | bytes 71743488 | tf_op jit(solution)/shard_map/qhd,khd->hqk/dot_general | solution.py:150
  348.9 30.1 %multiply_convert_fusion = bf16[12,832,832]{1,2,0:T(8,128)(2,1)} fusion(f32[12,832,832]{1,2,0:T(8,128)} %get-tuple-element.78, f32[12,832]{1,0:T(8,128)S(1)} %get-tuple-element.77, f32[12,832,832]{1,2,0:T(8,128)} %get-tuple-element.74, f32[12,832]{1,0:T(8,128)S(1)} %get-tuple-element.73), kind=kLoop, calls=%fused_computation.1 | loop fusion | flops 33226752 | bytes 83146752 | tf_op jit(solution)/shard_map/convert_element_type | solution.py:152
  382.7 10.4 %multiply_bitcast_fusion = bf16[832,12,64]{0,2,1:T(8,128)(2,1)} fusion(bf16[12,832,832]{1,2,0:T(8,128)(2,1)} %multiply_convert_fusion, bf16[832,12,192]{0,2,1:T(8,128)(2,1)} %bitcast.59), kind=kOutput, calls=%fused_computation.31 | convolution fusion | flops 1064534016 | bytes 20545536 | tf_op jit(solution)/shard_map/hqk,qhd->khd/dot_general | solution.py:154
  393.1 15.3 %fusion.23 = bf16[832,12,64]{0,2,1:T(8,128)(2,1)} fusion(bf16[832,12,64]{0,2,1:T(8,128)(2,1)S(1)} %bitcast.75, f32[12,832,832]{1,2,0:T(8,128)} %get-tuple-element.74, f32[12,832]{1,0:T(8,128)S(1)} %get-tuple-element.73), kind=kOutput, calls=%fused_computation.61 | convolution fusion | flops 1079869440 | bytes 35822592 | tf_op jit(solution)/shard_map/hqk,qhd->khd/dot_general | solution.py:155
  408.5 10.0 %multiply_bitcast_fusion.1 = bf16[832,12,64]{0,2,1:T(8,128)(2,1)S(1)} fusion(bf16[12,832,832]{1,2,0:T(8,128)(2,1)} %multiply_convert_fusion, bf16[832,12,192]{0,2,1:T(8,128)(2,1)} %bitcast.60), kind=kOutput, calls=%fused_computation.32 | convolution fusion | flops 1064534016 | bytes 20545536 | tf_op jit(solution)/shard_map/hqk,khd->qhd/dot_general | solution.py:153
  450.8 11.4 %multiply_reduce_fusion.4 = (f32[768]{0:T(1024)S(1)}, f32[832]{0:T(1024)S(1)}, f32[832]{0:T(1024)S(1)}, f32[768]{0:T(1024)S(1)}, f32[768]{0:T(1024)S(1)}, /*inde...) fusion(bf16[832,768]{1,0:T(8,128)(2,1)S(1)} %copy-done.3, f32[832]{0:T(1024)S(1)} %copy-done.30, ...), kind=kOutput, calls=%fused_computation.36 | convolution fusion | flops 2960371200 | bytes 18922240 | tf_op jit(solution)/shard_map/dot_general | solution.py:161
  465.2 64.2 %reduce-scatter.11.cloned.1.call-done = bf16[96,768]{1,0:T(8,128)(2,1)} async-done(((bf16[3072,768]{1,0:T(8,128)(2,1)}), bf16[96,768]{1,0:T(8,128)(2,1)}) %reduce-scatter.11.cloned.1.call-update) | async-done | bytes 147472 | tf_op jit(solution)/shard_map/reduce_scatter | solution.py:52
  529.7 18.5 %psum.14 = f32[12288]{0:T(1024)S(1)} all-reduce(f32[12288]{0:T(1024)S(1)} %constant_dynamic-update-slice_fusion), channel_id=1, replica_groups=mesh['dp'=8,'tp'=4] {'tp'}, use_global_device_ids=true, to_apply=%region_22.23 | all-reduce | flops 12288 | bytes 98304 | tf_op jit(solution)/shard_map/psum | solution.py:182
  548.2 22.7 %psum.15 = f32[12288]{0:T(1024)S(1)} all-reduce(f32[12288]{0:T(1024)S(1)} %psum.14), channel_id=1, replica_groups=mesh['dp'=8,'tp'=4] {'dp'}, use_global_device_ids=true, to_apply=%region_23.24 | all-reduce | flops 12288 | bytes 98304 | tf_op jit(solution)/shard_map/psum | solution.py:182
  576.4 54.0 %reduce-scatter.7.cloned.1.call-done = bf16[24,768]{1,0:T(8,128)(2,1)} async-done(((bf16[768,768]{1,0:T(8,128)(2,1)}), bf16[24,768]{1,0:T(8,128)(2,1)}) %reduce-scatter.7.cloned.1.call-update) | async-done | bytes 36880 | tf_op jit(solution)/shard_map/reduce_scatter | solution.py:52
  640.8 98.1 %reduce-scatter.13.cloned.1.call-done = bf16[96,576]{1,0:T(8,128)(2,1)} async-done(((bf16[3072,576]{1,0:T(8,128)(2,1)}), bf16[96,576]{1,0:T(8,128)(2,1)}) %reduce-scatter.13.cloned.1.call-update) | async-done | bytes 110608 | tf_op jit(solution)/shard_map/reduce_scatter | solution.py:52
  738.9 10.8 %all_gather.36 = bf16[768,576]{1,0:T(8,128)(2,1)S(1)} all-gather(bf16[96,576]{1,0:T(8,128)(2,1)} %reduce-scatter.13.cloned.1.call-done), channel_id=1, replica_groups=mesh['dp'=8,'tp'=4] {'dp'}, dimensions={0}, use_global_device_ids=true | all-gather | bytes 995328 | tf_op jit(solution)/shard_map/all_gather | solution.py:53
  751.7 12.1 %all-gather.17.cloned.1.call-done = bf16[768,768]{1,0:T(8,128)(2,1)} async-done(((bf16[96,768]{1,0:T(8,128)(2,1)}), bf16[768,768]{1,0:T(8,128)(2,1)}) %all-gather.17.cloned.1.call-update) | async-done | bytes 1179664 | tf_op jit(solution)/shard_map/all_gather | solution.py:53
  766.8 22.9 %all-gather.19.cloned.1.call-done = bf16[768,768]{1,0:T(8,128)(2,1)} async-done(((bf16[96,768]{1,0:T(8,128)(2,1)}), bf16[768,768]{1,0:T(8,128)(2,1)}) %all-gather.19.cloned.1.call-update) | async-done | bytes 1179664 | tf_op jit(solution)/shard_map/all_gather | solution.py:53
  (217 shorter events, 148.2 us)
Async XLA Ops:
  7.3 68.2 %all-gather.9.cloned.1.call-start = ((), (), s32[]{:S(2)}) async-start(), calls=%async_computation.4 | async-start | bytes 4055040 | tf_op jit(solution)/shard_map/all_gather | solution.py:47
  9.4 125.9 %all-gather.11.cloned.1.call-start = ((), (), s32[]{:S(2)}) async-start(), calls=%async_computation.5 | async-start | bytes 1216512 | tf_op jit(solution)/shard_map/all_gather | solution.py:47
  10.9 187.0 %all-gather.13.cloned.1.call-start = ((), (), s32[]{:S(2)}) async-start(), calls=%async_computation.6 | async-start | bytes 4866048 | tf_op jit(solution)/shard_map/all_gather | solution.py:47
  11.7 252.0 %all-gather.15.cloned.1.call-start = ((), (), s32[]{:S(2)}) async-start(), calls=%async_computation.7 | async-start | bytes 4866048 | tf_op jit(solution)/shard_map/all_gather | solution.py:47
  13.3 437.1 %reduce-scatter.9.cloned.1.call-start = ((), (), s32[]{:S(2)}) async-start(), calls=%async_computation.9 | async-start | bytes 4866048 | tf_op jit(solution)/shard_map/reduce_scatter | solution.py:52
  14.1 121.2 %copy-start.16 = (f32[832]{0:T(1024)}, f32[832]{0:T(1024)S(1)}, u32[]{:S(2)}) copy-start(f32[832]{0:T(1024)S(1)} %convert_element_type.150) | copy-start | bytes 9988
  15.4 295.8 %copy-start.14 = (f32[832]{0:T(1024)}, f32[832]{0:T(1024)S(1)}, u32[]{:S(2)}) copy-start(f32[832]{0:T(1024)S(1)} %convert_element_type.149) | copy-start | bytes 9988
  16.0 119.3 %copy-start.18 = (f32[832]{0:T(1024)}, f32[832]{0:T(1024)S(1)}, u32[]{:S(2)}) copy-start(f32[832]{0:T(1024)S(1)} %get-tuple-element.72) | copy-start | bytes 9988
  16.6 118.7 %copy-start.20 = (f32[768]{0:T(1024)}, f32[768]{0:T(1024)S(1)}, u32[]{:S(2)}) copy-start(f32[768]{0:T(1024)S(1)} %convert_element_type.151) | copy-start | bytes 9220
  16.6 69.4 %copy-start.27 = (f32[768]{0:T(1024)}, f32[768]{0:T(1024)S(1)}, u32[]{:S(2)}) copy-start(f32[768]{0:T(1024)S(1)} %convert_element_type.154) | copy-start | bytes 9220
  16.7 272.4 %copy-start.33 = (f32[768]{0:T(1024)}, f32[768]{0:T(1024)S(1)}, u32[]{:S(2)}) copy-start(f32[768]{0:T(1024)S(1)} %convert_element_type.163) | copy-start | bytes 9220
  16.7 69.3 %copy-start.35 = (f32[768]{0:T(1024)}, f32[768]{0:T(1024)S(1)}, u32[]{:S(2)}) copy-start(f32[768]{0:T(1024)S(1)} %convert_element_type.155) | copy-start | bytes 9220
  204.5 70.4 %slice-start = ((s8[4718592]{0:T(1024)(128)(4,1)}), s8[524288]{0:T(1024)(128)(4,1)S(1)}, s32[]{:S(2)}) async-start(s8[4718592]{0:T(1024)(128)(4,1)} %bitcast.65), calls=%async_computation.14 | async-start | bytes 1048576
  311.1 218.3 %reduce-scatter.11.cloned.1.call-start = ((), (), s32[]{:S(2)}) async-start(), calls=%async_computation.11 | async-start | bytes 4866048 | tf_op jit(solution)/shard_map/reduce_scatter | solution.py:52
  348.8 281.6 %reduce-scatter.7.cloned.1.call-start = ((), (), s32[]{:S(2)}) async-start(), calls=%async_computation.8 | async-start | bytes 1216512 | tf_op jit(solution)/shard_map/reduce_scatter | solution.py:52
  408.5 330.5 %reduce-scatter.13.cloned.1.call-start = ((), (), s32[]{:S(2)}) async-start(), calls=%async_computation.13 | async-start | bytes 4055040 | tf_op jit(solution)/shard_map/reduce_scatter | solution.py:52
  440.1 323.8 %all-gather.17.cloned.1.call-start = ((), (), s32[]{:S(2)}) async-start(), calls=%async_computation.10 | async-start | bytes 1327104 | tf_op jit(solution)/shard_map/all_gather | solution.py:53
  450.5 339.2 %all-gather.19.cloned.1.call-start = ((), (), s32[]{:S(2)}) async-start(), calls=%async_computation.12 | async-start | bytes 1327104 | tf_op jit(solution)/shard_map/all_gather | solution.py:53
  462.2 67.3 %copy-start.25 = (f32[768]{0:T(1024)S(1)}, f32[768]{0:T(1024)}, u32[]{:S(2)}) copy-start(f32[768]{0:T(1024)} %get-tuple-element.42) | copy-start | bytes 9220
  462.3 67.3 %copy-start.24 = (f32[768]{0:T(1024)S(1)}, f32[768]{0:T(1024)}, u32[]{:S(2)}) copy-start(f32[768]{0:T(1024)} %get-tuple-element.41) | copy-start | bytes 9220
  462.3 67.3 %copy-start.38 = (f32[768]{0:T(1024)S(1)}, f32[768]{0:T(1024)}, u32[]{:S(2)}) copy-start(f32[768]{0:T(1024)} %get-tuple-element.34) | copy-start | bytes 9220
  462.3 67.3 %copy-start.37 = (f32[768]{0:T(1024)S(1)}, f32[768]{0:T(1024)}, u32[]{:S(2)}) copy-start(f32[768]{0:T(1024)} %get-tuple-element.40) | copy-start | bytes 9220
  462.3 67.4 %copy-start.32 = (f32[3072]{0:T(1024)S(1)}, f32[3072]{0:T(1024)}, u32[]{:S(2)}) copy-start(f32[3072]{0:T(1024)} %get-tuple-element.82) | copy-start | bytes 36868
  462.3 110.7 %copy-start.31 = (f32[832]{0:T(1024)S(1)}, f32[832]{0:T(1024)}, u32[]{:S(2)}) copy-start(f32[832]{0:T(1024)} %get-tuple-element.71) | copy-start | bytes 9988
  (40 other events, 471.9 us)
Sparse Core Ops, SparseCore 0:
  11.6 63.8 all-gather.8
  79.0 52.7 all-gather.10
  135.2 62.5 all-gather.12
  201.2 62.4 all-gather.14
  311.2 105.7 reduce-scatter.8
  423.3 106.0 reduce-scatter.10
  535.1 95.3 reduce-scatter.6
  635.8 103.0 reduce-scatter.12
  740.8 22.9 all-gather.16
  765.6 24.0 all-gather.18
